TPU v7x, 256 devices: a whole 4x4x8 slice. The times are simulated.
256 devices in a mesh: rows: 64 (over y, z, core), cols: 4 (over x).
Axes of the slice: x: 4, y: 4, z: 8, core: 2. Of those that a mesh axis runs over, the one named last changes fastest.
Arguments:
- residual_block: float32 [524288, 64], P('rows', 'cols'), may hold values from -6 to 6
- basis: bfloat16 [524288, 64], P('rows', 'cols'), may hold values from -0.0078125 to 0.0078125
- fine_tiles: bfloat16 [4096, 4, 128, 128], P('rows')
- fine_index: int32 [4096, 4], P('rows'), may hold values from 0 to 4095, as said below
- mid_tiles: bfloat16 [512, 3, 128, 128], P('rows')
- fine_owner: int32 [524288], P('rows'), may hold values from 0 to 65535, as said below
- mid_owner: int32 [65536], P('rows'), may hold values from 0 to 8191, as said below
- coarse_inverse: float32 [8192, 8192], P('rows'), as said below
Outputs:
- directions: float32 [524288, 64], P('rows', 'cols')
- gram: float32 [64, 64], P(None, 'cols')
Inputs may be any that keep to these rules, and one draw needn't show every extreme that they name: `fine_index`: slot 0 of block row g names g itself; every block named in a block row of partition p (block rows p*64 to p*64 + 63) belongs to partition p - 1, p or p + 1. `fine_owner`: the fine vertices of partition p map to level-one rows p*1024 to p*1024 + 1023; every level-one row receives exactly 8 vertices. `mid_owner`: the level-one rows of partitions 2q and 2q + 1 map to level-two rows 2q*128 to 2q*128 + 2*128 - 1; every level-two row receives exactly 8 level-one rows. coarse_inverse is symmetric.
All inputs are finite; a program needn't handle non-finite values.
Results may differ from a plain program's by a relative error of at most 0.013.
Values may be sent and summed in bfloat16 or wider, within the bound.
A program may use at most 64 MiB of HBM per device.

v0:
```python
import jax
import jax.numpy as jnp
from jax import lax
from jax.sharding import PartitionSpec as P

DAMPING = 0.6666666666666666


def with_halo(array, sides, width):
    for axis, dim in sides:
        peers, length = (lax.axis_size(axis), array.shape[dim])
        up = [(i, (i + 1) % peers) for i in range(peers - 1)]
        down = [(j, i) for i, j in up]
        last = lax.slice_in_dim(array, length - width, length, axis=dim)
        leading = lax.slice_in_dim(array, 0, width, axis=dim)
        before = lax.ppermute(last, axis, up)
        after = lax.ppermute(leading, axis, down)
        array = jnp.concatenate([before, array, after], axis=dim)
    return array


def swapped(value, axis, apart):
    mask = 2**apart
    pairs = [(source, source ^ mask) for source in range(lax.axis_size(axis))]
    return lax.ppermute(value, axis, pairs)


def fine_apply(vector, matrix, window_index):
    extent = matrix.shape[2]
    packed = vector.astype(jnp.bfloat16).reshape(-1, extent, vector.shape[1])
    window = with_halo(packed, (("rows", 0),), packed.shape[0])
    picked = window[window_index]
    product = jnp.einsum("bkij,bkjc->bic", matrix, picked, preferred_element_type=jnp.float32)
    return product.reshape(vector.shape)


def mid_apply(vector, matrix):
    blocks = matrix.shape[0]
    extent = matrix.shape[2]
    packed = vector.astype(jnp.bfloat16).reshape(blocks, extent, vector.shape[1])
    window = with_halo(packed, (("rows", 0),), 1)
    product = jnp.einsum(
        "bij,bjc->bic", matrix[:, 0], window[:-2], preferred_element_type=jnp.float32
    )
    product = product + jnp.einsum(
        "bij,bjc->bic", matrix[:, 1], window[1:-1], preferred_element_type=jnp.float32
    )
    product = product + jnp.einsum(
        "bij,bjc->bic", matrix[:, 2], window[2:], preferred_element_type=jnp.float32
    )
    return product.reshape(vector.shape)


def on_device(
    residual_block, basis, fine_tiles, fine_index, mid_tiles, fine_owner, mid_owner, coarse_inverse
):
    device = lax.axis_index("rows")
    blocks = fine_tiles.shape[0]
    mid_count = mid_tiles.shape[0] * mid_tiles.shape[2]
    coarse_count = coarse_inverse.shape[0]
    col_width = residual_block.shape[1]
    parity = device % 2
    window_index = fine_index - (device - 1) * blocks
    fine_local = fine_owner - device * mid_count
    mid_local = mid_owner - (device - parity) * coarse_count
    fine_inv = 1.0 / jnp.diagonal(fine_tiles[:, 0], axis1=1, axis2=2).astype(jnp.float32).reshape(
        -1, 1
    )
    mid_inv = 1.0 / jnp.diagonal(mid_tiles[:, 1], axis1=1, axis2=2).astype(jnp.float32).reshape(
        -1, 1
    )
    fine_x = DAMPING * fine_inv * residual_block
    fine_x = fine_x + DAMPING * fine_inv * (
        residual_block - fine_apply(fine_x, fine_tiles, window_index)
    )
    fine_res = residual_block - fine_apply(fine_x, fine_tiles, window_index)
    partial_mid = jax.ops.segment_sum(fine_res, fine_local, num_segments=mid_count)
    mid_x = DAMPING * mid_inv * partial_mid
    mid_x = mid_x + DAMPING * mid_inv * (partial_mid - mid_apply(mid_x, mid_tiles))
    mid_res = partial_mid - mid_apply(mid_x, mid_tiles)
    partial_value = jax.ops.segment_sum(mid_res, mid_local, num_segments=2 * coarse_count)
    halves = partial_value.reshape(2, coarse_count, col_width)
    own_half = jnp.where(parity == 0, halves[0], halves[1])
    other_half = jnp.where(parity == 0, halves[1], halves[0])
    coarse_rhs = own_half + swapped(other_half, "rows", 0)
    coarse_fix = jnp.dot(
        coarse_inverse,
        lax.all_gather(coarse_rhs, "rows", axis=0, tiled=True),
        precision=lax.Precision.HIGHEST,
        preferred_element_type=jnp.float32,
    )
    partner_fix = swapped(coarse_fix, "rows", 0)
    pair_values = jnp.where(
        parity == 0,
        jnp.concatenate([coarse_fix, partner_fix], axis=0),
        jnp.concatenate([partner_fix, coarse_fix], axis=0),
    )
    mid_x = mid_x + pair_values[mid_local]
    mid_x = mid_x + DAMPING * mid_inv * (partial_mid - mid_apply(mid_x, mid_tiles))
    fine_x = fine_x + mid_x[fine_local]
    finished = fine_x + DAMPING * fine_inv * (
        residual_block - fine_apply(fine_x, fine_tiles, window_index)
    )
    rounded = finished.astype(jnp.bfloat16)
    partial_gram = lax.dot_general(
        lax.all_gather(basis, "cols", axis=1, tiled=True),
        rounded,
        (((0,), (0,)), ((), ())),
        preferred_element_type=jnp.float32,
    )
    gram = lax.psum(partial_gram, "rows")
    return (finished, gram)


def solution(mesh):
    in_specs = (
        P("rows", "cols"),
        P("rows", "cols"),
        P("rows", None, None, None),
        P("rows", None),
        P("rows", None, None, None),
        P("rows"),
        P("rows"),
        P("rows", None),
    )
    out_specs = (P("rows", "cols"), P(None, "cols"))
    return jax.shard_map(
        on_device, mesh=mesh, in_specs=in_specs, out_specs=out_specs, check_vma=False
    )
```

profile of v0, /device:TPU:4, one launch (start us, length us, event | category | flops | bytes accessed | tf_op | source)
XLA Modules:
  0.0 407.9 jit_solution(2754003155523653004)
XLA Ops:
  7.2 1.5 slice-done
  8.8 3.9 copy.204
  12.7 1.9 gather_fusion
  14.8 1.8 collective-permute-start
  16.5 1.3 collective-permute-start.1
  18.1 1.0 slice_bitcast_fusion
  19.1 3.1 copy.166
  22.2 1.9 gather_fusion.2
  24.3 0.8 gather_fusion.1
  25.2 5.7 %convolution_bitcast_fusion.2 = f32[64,2,8,128]{3,2,1,0:T(8,128)S(1)} fusion(bf16[64,4,128,16]{2,3,1,0:T(8,128)(2,1)S(1)} %bitcast.177, bf16[64,4,128,128]{3,2,1,0:T(8,128)(2,1)} %param.10), kind=kOutput, calls=%fused_computation.11 | convolution fusion | flops 134217728 | bytes 9961472 | tf_op jit(solution)/shard_map/bkij,bkjc->bic/dot_general | solution.py:33
  31.0 4.7 %collective-permute-start.2 = (bf16[64,128,16]{1,2,0:T(8,128)(2,1)S(1)}, bf16[64,128,16]{1,2,0:T(8,128)(2,1)S(1)}, u32[]{:S(2)}, u32[]{:S(2)}) collective-permute-start(bf16[64,128,16]{1,2,0:T(8,128)(2,1)S(1)} %copy_bitcast_fusion.1), channel_id=1, source_target_pairs={{0,4},{4,8},{8,12},{12,16},{16,20},{20,24},{24,28},{28,32},{32,36}... | collective-permute-start | bytes 786440 | tf_op jit(solution)/shard_map/ppermute | solution.py:16
  35.7 1.3 collective-permute-start.3
  37.1 3.3 collective-permute-done.3
  40.5 0.8 gather_fusion.3
  41.3 5.7 %convolution_bitcast_fusion.1 = f32[64,2,8,128]{3,2,1,0:T(8,128)S(1)} fusion(bf16[64,4,128,16]{2,3,1,0:T(8,128)(2,1)S(1)} %bitcast.178, bf16[64,4,128,128]{3,2,1,0:T(8,128)(2,1)} %param.10), kind=kOutput, calls=%fused_computation.10 | convolution fusion | flops 134217728 | bytes 9961472 | tf_op jit(solution)/shard_map/bkij,bkjc->bic/dot_general | solution.py:33
  47.1 2.6 copy.172
  49.7 44.4 %scatter_custom_fusion = f32[1024,16]{1,0:T(8,128)S(1)} fusion(s32[8192]{0:T(1024)S(1)} %get-tuple-element.11, f32[8192,16]{1,0:T(8,128)} %copy.172, f32[]{:T(128)} %constant.25.clone.1), kind=kCustom, calls=%fused_computation.51 | custom fusion | flops 131072 | bytes 66048 | tf_op jit(solution)/shard_map/scatter-add | solution.py:77
  94.3 0.2 fusion.65
  94.6 1.3 collective-permute-start.5
  95.9 7.3 %collective-permute-start.4 = (bf16[1,128,16]{1,2,0:T(8,128)(2,1)S(1)}, bf16[1,128,16]{1,2,0:T(8,128)(2,1)S(1)}, u32[]{:S(2)}, u32[]{:S(2)}) collective-permute-start(bf16[1,128,16]{1,2,0:T(8,128)(2,1)S(1)} %get-tuple-element.18), channel_id=1, source_target_pairs={{0,4},{4,8},{8,12},{12,16},{16,20},{20,24},{24,28},{28,32},{32,36}... | collective-permute-start | bytes 12296 | tf_op jit(solution)/shard_map/ppermute | solution.py:16
  103.4 0.6 collective-permute-done.4
  104.3 0.2 fusion.66
  104.5 1.3 collective-permute-start.7
  105.8 4.2 %collective-permute-start.6 = (bf16[1,128,16]{1,2,0:T(8,128)(2,1)S(1)}, bf16[1,128,16]{1,2,0:T(8,128)(2,1)S(1)}, u32[]{:S(2)}, u32[]{:S(2)}) collective-permute-start(bf16[1,128,16]{1,2,0:T(8,128)(2,1)S(1)} %get-tuple-element.16), channel_id=1, source_target_pairs={{0,4},{4,8},{8,12},{12,16},{16,20},{20,24},{24,28},{28,32},{32,36}... | collective-permute-start | bytes 12296 | tf_op jit(solution)/shard_map/ppermute | solution.py:16
  110.3 0.6 collective-permute-done.6
  111.3 0.9 bitcast_subtract_fusion.3
  112.2 6.4 %scatter_custom_fusion.1 = f32[256,16]{1,0:T(8,128)S(1)} fusion(s32[1024]{0:T(1024)S(1)} %get-tuple-element.13, f32[1024,16]{1,0:T(8,128)} %bitcast_subtract_fusion.3, f32[]{:T(128)} %constant.25.clone.1), kind=kCustom, calls=%fused_computation.70 | custom fusion | flops 16384 | bytes 16896 | tf_op jit(solution)/shard_map/scatter-add | solution.py:81
  118.6 2.5 collective-permute-start.8
  121.1 0.9 collective-permute-done.8
  122.0 65.2 %all_gather.6 = f32[8192,16]{1,0:T(8,128)S(1)} all-gather(f32[128,16]{1,0:T(8,128)S(1)} %select_add_fusion), channel_id=1, replica_groups=mesh['rows'=64,'cols'=4] {'rows'}, dimensions={0}, use_global_device_ids=true | all-gather | bytes 532480 | tf_op jit(solution)/shard_map/all_gather | solution.py:88
  187.2 6.6 %convolution_bitcast_fusion.4 = f32[128,16]{0,1:T(8,128)S(1)} fusion(f32[8192,16]{1,0:T(8,128)S(1)} %all_gather.6, f32[128,8192]{1,0:T(8,128)S(1)} %copy-done.2), kind=kOutput, calls=%fused_computation.22 | convolution fusion | flops 201326592 | bytes 4726784 | tf_op jit(solution)/shard_map/dot_general | solution.py:86
  193.8 0.4 collective-permute-start.9
  194.2 0.8 collective-permute-done.9
  195.1 2.8 gather_fusion.4
  198.2 0.2 fusion.67
  198.4 1.3 collective-permute-start.11
  199.7 3.0 collective-permute-start.10
  203.0 0.6 collective-permute-done.10
  204.0 27.9 %gather_fusion.5 = f32[8192,16]{1,0:T(8,128)} fusion(f32[1024,16]{1,0:T(8,128)S(1)} %copy.193, s32[8192]{0:T(1024)S(1)} %get-tuple-element.10), kind=kCustom, calls=%fused_computation.5 | custom fusion | bytes 1081344 | tf_op jit(solution)/shard_map/gather | solution.py:100
  231.9 2.8 copy.194
  234.8 3.4 collective-permute-start.12
  238.3 1.3 collective-permute-start.13
  239.6 3.9 collective-permute-done.13
  243.6 0.8 gather_fusion.6
  244.4 5.7 %convolution_bitcast_fusion = f32[64,2,8,128]{3,2,1,0:T(8,128)S(1)} fusion(bf16[64,4,128,16]{2,3,1,0:T(8,128)(2,1)S(1)} %bitcast.176, bf16[64,4,128,128]{3,2,1,0:T(8,128)(2,1)} %param.10), kind=kOutput, calls=%fused_computation.9 | convolution fusion | flops 134217728 | bytes 9961472 | tf_op jit(solution)/shard_map/bkij,bkjc->bic/dot_general | solution.py:33
  250.3 18.4 %all-gather.2.cloned.1.call-done = bf16[8192,64]{0,1:T(8,128)(2,1)} async-done(((bf16[8192,16]{0,1:T(8,128)(2,1)}), bf16[8192,64]{0,1:T(8,128)(2,1)}) %all-gather.2.cloned.1.call-update) | async-done | bytes 1048592 | tf_op jit(solution)/shard_map/all_gather | solution.py:106
  268.7 1.6 convolution_bitcast_fusion.3
  270.3 130.8 %psum.7 = f32[64,16]{0,1:T(8,128)} all-reduce(f32[64,16]{0,1:T(8,128)S(1)} %convolution_bitcast_fusion.3), channel_id=1, replica_groups=mesh['rows'=64,'cols'=4] {'rows'}, use_global_device_ids=true, to_apply=%region_2.3 | all-reduce | flops 1024 | bytes 8192 | tf_op jit(solution)/shard_map/psum | solution.py:111
  (67 shorter events, 3.8 us)
Async XLA Ops:
  7.2 1.6 slice-start
  7.2 261.5 %all-gather.2.cloned.1.call-start = ((), (), s32[]{:S(2)}) async-start(), calls=%async_computation | async-start | bytes 1310720 | tf_op jit(solution)/shard_map/all_gather | solution.py:106
  8.8 6.0 %copy-start = (f32[8192,16]{0,1:T(8,128)S(1)}, f32[8192,16]{0,1:T(8,128)}, u32[]{:S(2)}) copy-start(f32[8192,16]{0,1:T(8,128)} %param.8) | copy-start | bytes 1572868
  8.8 9.1 %copy-start.6 = (s32[64,4]{0,1:T(4,128)S(1)}, s32[64,4]{0,1:T(4,128)}, u32[]{:S(2)}) copy-start(s32[64,4]{0,1:T(4,128)} %param.11) | copy-start | bytes 3076
  12.7 11.5 %copy-start.5 = (s32[1024]{0:T(1024)S(1)}, s32[1024]{0:T(1024)}, u32[]{:S(2)}) copy-start(s32[1024]{0:T(1024)} %param.14) | copy-start | bytes 12292
  14.8 9.4 %collective-permute-start = (bf16[64,128,16]{1,2,0:T(8,128)(2,1)S(1)}, bf16[64,128,16]{1,2,0:T(8,128)(2,1)S(1)}, u32[]{:S(2)}, u32[]{:S(2)}) collective-permute-start(bf16[64,128,16]{1,2,0:T(8,128)(2,1)S(1)} %copy_bitcast_fusion.2), channel_id=1, source_target_pairs={{0,4},{4,8},{8,12},{12,16},{16,20},{20,24},{24,28},{28,32},{32,36}... | collective-permute-start | bytes 786440 | tf_op jit(solution)/shard_map/ppermute | solution.py:16
  16.5 7.7 %collective-permute-start.1 = (bf16[64,128,16]{1,2,0:T(8,128)(2,1)S(1)}, bf16[64,128,16]{1,2,0:T(8,128)(2,1)S(1)}, u32[]{:S(2)}, u32[]{:S(2)}) collective-permute-start(bf16[64,128,16]{1,2,0:T(8,128)(2,1)S(1)} %copy_bitcast_fusion.2), channel_id=1, source_target_pairs={{4,0},{8,4},{12,8},{16,12},{20,16},{24,20},{28,24},{32,28},{36,32}... | collective-permute-start | bytes 786440 | tf_op jit(solution)/shard_map/ppermute | solution.py:17
  25.2 11.9 %copy-start.4 = (s32[8192]{0:T(1024)S(1)}, s32[8192]{0:T(1024)}, u32[]{:S(2)}) copy-start(s32[8192]{0:T(1024)} %param.13) | copy-start | bytes 98308
  31.0 6.1 %collective-permute-start.2 = (bf16[64,128,16]{1,2,0:T(8,128)(2,1)S(1)}, bf16[64,128,16]{1,2,0:T(8,128)(2,1)S(1)}, u32[]{:S(2)}, u32[]{:S(2)}) collective-permute-start(bf16[64,128,16]{1,2,0:T(8,128)(2,1)S(1)} %copy_bitcast_fusion.1), channel_id=1, source_target_pairs={{0,4},{4,8},{8,12},{12,16},{16,20},{20,24},{24,28},{28,32},{32,36}... | collective-permute-start | bytes 786440 | tf_op jit(solution)/shard_map/ppermute | solution.py:16
  35.7 4.7 %collective-permute-start.3 = (bf16[64,128,16]{1,2,0:T(8,128)(2,1)S(1)}, bf16[64,128,16]{1,2,0:T(8,128)(2,1)S(1)}, u32[]{:S(2)}, u32[]{:S(2)}) collective-permute-start(bf16[64,128,16]{1,2,0:T(8,128)(2,1)S(1)} %copy_bitcast_fusion.1), channel_id=1, source_target_pairs={{4,0},{8,4},{12,8},{16,12},{20,16},{24,20},{28,24},{32,28},{36,32}... | collective-permute-start | bytes 786440 | tf_op jit(solution)/shard_map/ppermute | solution.py:17
  47.0 47.3 %copy-start.1 = (bf16[8,3,128,128]{3,2,1,0:T(8,128)(2,1)S(1)}, bf16[8,3,128,128]{3,2,1,0:T(8,128)(2,1)}, u32[]{:S(2)}) copy-start(bf16[8,3,128,128]{3,2,1,0:T(8,128)(2,1)} %param.12) | copy-start | bytes 2359300
  94.6 8.6 %collective-permute-start.5 = (bf16[1,128,16]{1,2,0:T(8,128)(2,1)S(1)}, bf16[1,128,16]{1,2,0:T(8,128)(2,1)S(1)}, u32[]{:S(2)}, u32[]{:S(2)}) collective-permute-start(bf16[1,128,16]{1,2,0:T(8,128)(2,1)S(1)} %get-tuple-element.19), channel_id=1, source_target_pairs={{4,0},{8,4},{12,8},{16,12},{20,16},{24,20},{28,24},{32,28},{36,32}... | collective-permute-start | bytes 12296 | tf_op jit(solution)/shard_map/ppermute | solution.py:17
  95.9 8.1 %collective-permute-start.4 = (bf16[1,128,16]{1,2,0:T(8,128)(2,1)S(1)}, bf16[1,128,16]{1,2,0:T(8,128)(2,1)S(1)}, u32[]{:S(2)}, u32[]{:S(2)}) collective-permute-start(bf16[1,128,16]{1,2,0:T(8,128)(2,1)S(1)} %get-tuple-element.18), channel_id=1, source_target_pairs={{0,4},{4,8},{8,12},{12,16},{16,20},{20,24},{24,28},{28,32},{32,36}... | collective-permute-start | bytes 12296 | tf_op jit(solution)/shard_map/ppermute | solution.py:16
  104.5 5.5 %collective-permute-start.7 = (bf16[1,128,16]{1,2,0:T(8,128)(2,1)S(1)}, bf16[1,128,16]{1,2,0:T(8,128)(2,1)S(1)}, u32[]{:S(2)}, u32[]{:S(2)}) collective-permute-start(bf16[1,128,16]{1,2,0:T(8,128)(2,1)S(1)} %get-tuple-element.17), channel_id=1, source_target_pairs={{4,0},{8,4},{12,8},{16,12},{20,16},{24,20},{28,24},{32,28},{36,32}... | collective-permute-start | bytes 12296 | tf_op jit(solution)/shard_map/ppermute | solution.py:17
  105.8 5.0 %collective-permute-start.6 = (bf16[1,128,16]{1,2,0:T(8,128)(2,1)S(1)}, bf16[1,128,16]{1,2,0:T(8,128)(2,1)S(1)}, u32[]{:S(2)}, u32[]{:S(2)}) collective-permute-start(bf16[1,128,16]{1,2,0:T(8,128)(2,1)S(1)} %get-tuple-element.16), channel_id=1, source_target_pairs={{0,4},{4,8},{8,12},{12,16},{16,20},{20,24},{24,28},{28,32},{32,36}... | collective-permute-start | bytes 12296 | tf_op jit(solution)/shard_map/ppermute | solution.py:16
  118.6 68.6 %copy-start.2 = (f32[128,8192]{1,0:T(8,128)S(1)}, f32[128,8192]{1,0:T(8,128)}, u32[]{:S(2)}) copy-start(f32[128,8192]{1,0:T(8,128)} %param.15) | copy-start | bytes 12582916
  118.6 3.4 collective-permute-start.8
  193.8 1.2 collective-permute-start.9
  198.4 4.4 %collective-permute-start.11 = (bf16[1,128,16]{1,2,0:T(8,128)(2,1)S(1)}, bf16[1,128,16]{1,2,0:T(8,128)(2,1)S(1)}, u32[]{:S(2)}, u32[]{:S(2)}) collective-permute-start(bf16[1,128,16]{1,2,0:T(8,128)(2,1)S(1)} %get-tuple-element.15), channel_id=1, source_target_pairs={{4,0},{8,4},{12,8},{16,12},{20,16},{24,20},{28,24},{32,28},{36,32}... | collective-permute-start | bytes 12296 | tf_op jit(solution)/shard_map/ppermute | solution.py:17
  199.7 3.8 collective-permute-start.10
  234.8 4.8 %collective-permute-start.12 = (bf16[64,128,16]{1,2,0:T(8,128)(2,1)S(1)}, bf16[64,128,16]{1,2,0:T(8,128)(2,1)S(1)}, u32[]{:S(2)}, u32[]{:S(2)}) collective-permute-start(bf16[64,128,16]{1,2,0:T(8,128)(2,1)S(1)} %copy_bitcast_fusion), channel_id=1, source_target_pairs={{0,4},{4,8},{8,12},{12,16},{16,20},{20,24},{24,28},{28,32},{32,36}... | collective-permute-start | bytes 786440 | tf_op jit(solution)/shard_map/ppermute | solution.py:16
  238.3 5.2 %collective-permute-start.13 = (bf16[64,128,16]{1,2,0:T(8,128)(2,1)S(1)}, bf16[64,128,16]{1,2,0:T(8,128)(2,1)S(1)}, u32[]{:S(2)}, u32[]{:S(2)}) collective-permute-start(bf16[64,128,16]{1,2,0:T(8,128)(2,1)S(1)} %copy_bitcast_fusion), channel_id=1, source_target_pairs={{4,0},{8,4},{12,8},{16,12},{20,16},{24,20},{28,24},{32,28},{36,32}... | collective-permute-start | bytes 786440 | tf_op jit(solution)/shard_map/ppermute | solution.py:17
  250.3 150.8 %copy-start.3 = (f32[8192,16]{0,1:T(8,128)}, f32[8192,16]{0,1:T(8,128)S(1)}, u32[]{:S(2)}) copy-start(f32[8192,16]{0,1:T(8,128)S(1)} %fusion.7) | copy-start | bytes 1572868
Sparse Core Ops, SparseCore 0:
  239.7 28.9 all-gather.1
where the time goes:
time: 409 us; the launch traced here: 408 us
  blocking collectives  196 us (48%)
  local copies, waits for them, and re-layouts  53.3 us (13%)
  other arithmetic  52.8 us (13%)
  starting transfers between devices  35.1 us (9%)
  waiting for transfers between devices  29 us (7%)
  matrix products  27.3 us (7%)
  between operations  14.5 us (4%)
    psum x1, blocking collectives, on_device(): gram = lax.psum(partial_gram, 'rows')  131 us
    all_gather x1, blocking collectives, on_device(): lax.all_gather(coarse_rhs, 'rows', axis=0, tiled=True)  65.2 us
    scatter-add x1, other arithmetic, on_device(): jax.ops.segment_sum(fine_res, fine_local, num_segments=mid_count)  44.4 us
    gather x2, local copies, waits for them, and re-layouts, on_device(): fine_x = fine_x + mid_x[fine_local]  30.7 us
    ppermute x6, starting transfers between devices, with_halo(): before = lax.ppermute(last, axis, up)  24.4 us
    all_gather x1, waiting for transfers between devices, on_device(): lax.all_gather(basis, 'cols', axis=1, tiled=True)  18.4 us
    dot_general x3, matrix products, fine_apply(): jnp.einsum('bkij,bkjc->bic', matrix, picked, preferred_element_type=jnp.f...  17 us
  transfers between devices with their start and end apart: 15, of which 8 were waited for; matrix products, arithmetic and copies ran while one was open for 3% of the time, Pallas kernels for 0%

commit v1 on v0

--- a/solution.py
+++ b/solution.py
@@ -4,6 +4,33 @@
 from jax.sharding import PartitionSpec as P
 
 DAMPING = 0.6666666666666666
+
+
+def guide_heaps(tile_in, axis_id, where_dim):
+    z_new = lax.psum(1, axis_id)
+    val2 = lax.axis_index(axis_id)
+    w1, s_next, seen_now = (z_new, val2, tile_in.shape[where_dim])
+    tray = [(pp, (pp + 1) % w1) for pp in range(w1)]
+    main = jnp.zeros(
+        (*tile_in.shape[:where_dim], w1 * seen_now, *tile_in.shape[where_dim + 1 :]), tile_in.dtype
+    )
+    seen = [(pp, (pp - 1) % w1) for pp in range(w1)]
+    main = lax.dynamic_update_slice_in_dim(main, tile_in, s_next * seen_now, axis=where_dim)
+    outcome_arr = w1 // 2
+    kk = 1
+    all_values = b_now = tile_in
+    while kk < outcome_arr + 1:
+        all_values = lax.ppermute(all_values, axis_id, tray)
+        main = lax.dynamic_update_slice_in_dim(
+            main, all_values, (s_next - kk) % w1 * seen_now, axis=where_dim
+        )
+        if kk < w1 - outcome_arr:
+            b_now = lax.ppermute(b_now, axis_id, seen)
+            main = lax.dynamic_update_slice_in_dim(
+                main, b_now, (s_next + kk) % w1 * seen_now, axis=where_dim
+            )
+        kk += 1
+    return main
 
 
 def with_halo(array, sides, width):
@@ -103,7 +130,7 @@
     )
     rounded = finished.astype(jnp.bfloat16)
     partial_gram = lax.dot_general(
-        lax.all_gather(basis, "cols", axis=1, tiled=True),
+        guide_heaps(basis, "cols", where_dim=1),
         rounded,
         (((0,), (0,)), ((), ())),
         preferred_element_type=jnp.float32,

time: 409 us -> 381 us (0.932)
  waiting for transfers between devices: 29 us -> 6.02 us
  between operations: 14.5 us -> 1.22 us
  local copies, waits for them, and re-layouts: 53.3 us -> 59.4 us
    all_gather x1 -> x0, waiting for transfers between devices: 18.4 us -> none  [on_device(): lax.all_gather(basis, 'cols', axis=1, tiled=True)]
    dynamic_update_slice x0 -> x4, local copies, waits for them, and re-layouts: none -> 6.05 us  [the longest x2 3.38 us: guide_heaps(): lax.dynamic_update_slice_in_dim(main, all_values, (s_next - kk) % w1 * se...]
  transfers between devices with their start and end apart: 15 -> 17, of which waited for: 8 -> 5; matrix products, arithmetic and copies ran while one was open for 3% -> 32% of each run, Pallas kernels for 0% -> 0%
where the time goes in v1:
time: 381 us; the launch traced here: 380 us
  blocking collectives  196 us (51%)
  local copies, waits for them, and re-layouts  59.4 us (16%)
  other arithmetic  52.8 us (14%)
  starting transfers between devices  37.9 us (10%)
  matrix products  26.2 us (7%)
  waiting for transfers between devices  6.02 us (2%)
    psum x1, blocking collectives, on_device(): gram = lax.psum(partial_gram, 'rows')  131 us
    all_gather x1, blocking collectives, on_device(): lax.all_gather(coarse_rhs, 'rows', axis=0, tiled=True)  65.1 us
    scatter-add x1, other arithmetic, on_device(): jax.ops.segment_sum(fine_res, fine_local, num_segments=mid_count)  44.4 us
    gather x2, local copies, waits for them, and re-layouts, on_device(): fine_x = fine_x + mid_x[fine_local]  30.6 us
    ppermute x6, starting transfers between devices, with_halo(): before = lax.ppermute(last, axis, up)  24.1 us
    dot_general x3, matrix products, fine_apply(): jnp.einsum('bkij,bkjc->bic', matrix, picked, preferred_element_type=jnp.f...  17.1 us
    ppermute x6, starting transfers between devices, with_halo(): after = lax.ppermute(leading, axis, down)  7.78 us
  transfers between devices with their start and end apart: 17, of which 5 were waited for; matrix products, arithmetic and copies ran while one was open for 32% of the time, Pallas kernels for 0%

profile of v1, /device:TPU:4, one launch (start us, length us, event | category | flops | bytes accessed | tf_op | source)
XLA Modules:
  0.0 380.0 jit_solution(5236980980485462611)
XLA Ops:
  0.7 1.6 slice-done
  2.2 3.9 %copy.204 = bf16[64,1,128,128]{0,3,2,1:T(8,128)(2,1)} copy(bf16[64,1,128,128]{3,2,1,0:T(8,128)(2,1)S(1)} %slice-done) | data formatting | bytes 4194304
  6.1 2.0 gather_fusion
  8.3 1.8 collective-permute-start
  10.0 1.3 collective-permute-start.1
  11.3 1.3 collective-permute-start.14
  12.6 0.8 collective-permute-start.15
  13.6 1.0 slice_bitcast_fusion
  14.7 1.0 constant_dynamic-update-slice_fusion.3
  15.7 3.1 copy.166
  18.8 2.0 gather_fusion.2
  21.0 0.8 gather_fusion.1
  21.8 5.7 %convolution_bitcast_fusion.2 = f32[64,2,8,128]{3,2,1,0:T(8,128)S(1)} fusion(bf16[64,4,128,16]{2,3,1,0:T(8,128)(2,1)S(1)} %bitcast.175, bf16[64,4,128,128]{3,2,1,0:T(8,128)(2,1)} %param.10), kind=kOutput, calls=%fused_computation.11 | convolution fusion | flops 134217728 | bytes 9961472 | tf_op jit(solution)/shard_map/bkij,bkjc->bic/dot_general | solution.py:60
  27.6 4.2 %collective-permute-start.2 = (bf16[64,128,16]{1,2,0:T(8,128)(2,1)S(1)}, bf16[64,128,16]{1,2,0:T(8,128)(2,1)S(1)}, u32[]{:S(2)}, u32[]{:S(2)}) collective-permute-start(bf16[64,128,16]{1,2,0:T(8,128)(2,1)S(1)} %copy_bitcast_fusion.1), channel_id=1, source_target_pairs={{0,4},{4,8},{8,12},{12,16},{16,20},{20,24},{24,28},{28,32},{32,36}... | collective-permute-start | bytes 786440 | tf_op jit(solution)/shard_map/ppermute | solution.py:43
  31.8 1.3 collective-permute-start.3
  33.2 1.3 collective-permute-start.16
  34.5 2.5 collective-permute-done.3
  37.1 0.8 gather_fusion.3
  38.0 5.7 %convolution_bitcast_fusion.1 = f32[64,2,8,128]{3,2,1,0:T(8,128)S(1)} fusion(bf16[64,4,128,16]{2,3,1,0:T(8,128)(2,1)S(1)} %bitcast.176, bf16[64,4,128,128]{3,2,1,0:T(8,128)(2,1)} %param.10), kind=kOutput, calls=%fused_computation.10 | convolution fusion | flops 134217728 | bytes 9961472 | tf_op jit(solution)/shard_map/bkij,bkjc->bic/dot_general | solution.py:60
  43.7 2.6 copy.172
  46.3 44.4 %scatter_custom_fusion = f32[1024,16]{1,0:T(8,128)S(1)} fusion(s32[8192]{0:T(1024)S(1)} %get-tuple-element.11, f32[8192,16]{1,0:T(8,128)} %copy.172, f32[]{:T(128)} %constant.71.clone.1), kind=kCustom, calls=%fused_computation.51 | custom fusion | flops 131072 | bytes 66048 | tf_op jit(solution)/shard_map/scatter-add | solution.py:104
  91.2 1.3 collective-permute-start.5
  92.5 7.3 %collective-permute-start.4 = (bf16[1,128,16]{1,2,0:T(8,128)(2,1)S(1)}, bf16[1,128,16]{1,2,0:T(8,128)(2,1)S(1)}, u32[]{:S(2)}, u32[]{:S(2)}) collective-permute-start(bf16[1,128,16]{1,2,0:T(8,128)(2,1)S(1)} %get-tuple-element.18), channel_id=1, source_target_pairs={{0,4},{4,8},{8,12},{12,16},{16,20},{20,24},{24,28},{28,32},{32,36}... | collective-permute-start | bytes 12296 | tf_op jit(solution)/shard_map/ppermute | solution.py:43
  100.1 0.6 collective-permute-done.4
  101.2 1.3 collective-permute-start.7
  102.5 4.4 %collective-permute-start.6 = (bf16[1,128,16]{1,2,0:T(8,128)(2,1)S(1)}, bf16[1,128,16]{1,2,0:T(8,128)(2,1)S(1)}, u32[]{:S(2)}, u32[]{:S(2)}) collective-permute-start(bf16[1,128,16]{1,2,0:T(8,128)(2,1)S(1)} %get-tuple-element.16), channel_id=1, source_target_pairs={{0,4},{4,8},{8,12},{12,16},{16,20},{20,24},{24,28},{28,32},{32,36}... | collective-permute-start | bytes 12296 | tf_op jit(solution)/shard_map/ppermute | solution.py:43
  107.1 0.4 collective-permute-done.6
  107.9 0.9 bitcast_subtract_fusion.3
  108.8 6.4 %scatter_custom_fusion.1 = f32[256,16]{1,0:T(8,128)S(1)} fusion(s32[1024]{0:T(1024)S(1)} %get-tuple-element.13, f32[1024,16]{1,0:T(8,128)} %bitcast_subtract_fusion.3, f32[]{:T(128)} %constant.71.clone.1), kind=kCustom, calls=%fused_computation.70 | custom fusion | flops 16384 | bytes 16896 | tf_op jit(solution)/shard_map/scatter-add | solution.py:108
  115.3 2.3 collective-permute-start.8
  117.6 1.7 constant_dynamic-update-slice_fusion.2
  119.3 65.1 %all_gather.3 = f32[8192,16]{1,0:T(8,128)S(1)} all-gather(f32[128,16]{1,0:T(8,128)S(1)} %select_add_fusion), channel_id=1, replica_groups=mesh['rows'=64,'cols'=4] {'rows'}, dimensions={0}, use_global_device_ids=true | all-gather | bytes 532480 | tf_op jit(solution)/shard_map/all_gather | solution.py:115
  184.4 6.6 %convolution_bitcast_fusion.3 = f32[128,16]{0,1:T(8,128)S(1)} fusion(f32[8192,16]{1,0:T(8,128)S(1)} %all_gather.3, f32[128,8192]{1,0:T(8,128)S(1)} %copy-done.2), kind=kOutput, calls=%fused_computation.21 | convolution fusion | flops 201326592 | bytes 4726784 | tf_op jit(solution)/shard_map/dot_general | solution.py:113
  191.0 0.4 collective-permute-start.9
  191.3 1.7 constant_dynamic-update-slice_fusion.1
  193.1 2.8 gather_fusion.4
  196.4 1.3 collective-permute-start.11
  197.7 3.3 collective-permute-start.10
  202.0 27.8 %gather_fusion.5 = f32[8192,16]{1,0:T(8,128)} fusion(f32[1024,16]{1,0:T(8,128)S(1)} %copy.193, s32[8192]{0:T(1024)S(1)} %get-tuple-element.10), kind=kCustom, calls=%fused_computation.5 | custom fusion | bytes 1081344 | tf_op jit(solution)/shard_map/gather | solution.py:127
  229.9 2.8 copy.194
  232.8 3.2 collective-permute-start.12
  236.1 1.3 collective-permute-start.13
  237.4 1.7 constant_dynamic-update-slice_fusion
  239.1 2.2 collective-permute-done.13
  241.4 0.8 gather_fusion.6
  242.2 5.7 %convolution_bitcast_fusion = f32[64,2,8,128]{3,2,1,0:T(8,128)S(1)} fusion(bf16[64,4,128,16]{2,3,1,0:T(8,128)(2,1)S(1)} %bitcast.174, bf16[64,4,128,128]{3,2,1,0:T(8,128)(2,1)} %param.10), kind=kOutput, calls=%fused_computation.9 | convolution fusion | flops 134217728 | bytes 9961472 | tf_op jit(solution)/shard_map/bkij,bkjc->bic/dot_general | solution.py:60
  248.2 0.4 fusion.20
  248.6 131.4 %psum.7 = f32[64,16]{0,1:T(8,128)} all-reduce(f32[64,16]{0,1:T(8,128)S(1)} %fusion.20), channel_id=1, replica_groups=mesh['rows'=64,'cols'=4] {'rows'}, use_global_device_ids=true, to_apply=%region_2.3 | all-reduce | flops 1024 | bytes 8192 | tf_op jit(solution)/shard_map/psum | solution.py:138
  (79 shorter events, 4.8 us)
Async XLA Ops:
  0.6 1.6 slice-start
  2.2 6.0 %copy-start = (f32[8192,16]{0,1:T(8,128)S(1)}, f32[8192,16]{0,1:T(8,128)}, u32[]{:S(2)}) copy-start(f32[8192,16]{0,1:T(8,128)} %param.8) | copy-start | bytes 1572868
  2.2 11.2 %copy-start.8 = (s32[64,4]{0,1:T(4,128)S(1)}, s32[64,4]{0,1:T(4,128)}, u32[]{:S(2)}) copy-start(s32[64,4]{0,1:T(4,128)} %param.11) | copy-start | bytes 3076
  6.1 14.7 %copy-start.7 = (s32[1024]{0:T(1024)S(1)}, s32[1024]{0:T(1024)}, u32[]{:S(2)}) copy-start(s32[1024]{0:T(1024)} %param.14) | copy-start | bytes 12292
  8.3 12.6 %collective-permute-start = (bf16[64,128,16]{1,2,0:T(8,128)(2,1)S(1)}, bf16[64,128,16]{1,2,0:T(8,128)(2,1)S(1)}, u32[]{:S(2)}, u32[]{:S(2)}) collective-permute-start(bf16[64,128,16]{1,2,0:T(8,128)(2,1)S(1)} %copy_bitcast_fusion.2), channel_id=1, source_target_pairs={{0,4},{4,8},{8,12},{12,16},{16,20},{20,24},{24,28},{28,32},{32,36}... | collective-permute-start | bytes 786440 | tf_op jit(solution)/shard_map/ppermute | solution.py:43
  10.0 10.9 %collective-permute-start.1 = (bf16[64,128,16]{1,2,0:T(8,128)(2,1)S(1)}, bf16[64,128,16]{1,2,0:T(8,128)(2,1)S(1)}, u32[]{:S(2)}, u32[]{:S(2)}) collective-permute-start(bf16[64,128,16]{1,2,0:T(8,128)(2,1)S(1)} %copy_bitcast_fusion.2), channel_id=1, source_target_pairs={{4,0},{8,4},{12,8},{16,12},{20,16},{24,20},{28,24},{32,28},{36,32}... | collective-permute-start | bytes 786440 | tf_op jit(solution)/shard_map/ppermute | solution.py:44
  11.3 21.9 %collective-permute-start.14 = (bf16[8192,16]{0,1:T(8,128)(2,1)}, bf16[8192,16]{0,1:T(8,128)(2,1)}, u32[]{:S(2)}, u32[]{:S(2)}) collective-permute-start(bf16[8192,16]{0,1:T(8,128)(2,1)} %param.9), channel_id=1, source_target_pairs={{0,1},{1,2},{2,3},{3,0},{4,5},{5,6},{6,7},{7,4},{8,9},{9,10},{10,1... | collective-permute-start | bytes 786440 | tf_op jit(solution)/shard_map/ppermute | solution.py:23
  12.6 178.7 %collective-permute-start.15 = (bf16[8192,16]{0,1:T(8,128)(2,1)}, bf16[8192,16]{0,1:T(8,128)(2,1)}, u32[]{:S(2)}, u32[]{:S(2)}) collective-permute-start(bf16[8192,16]{0,1:T(8,128)(2,1)} %param.9), channel_id=1, source_target_pairs={{0,3},{1,0},{2,1},{3,2},{4,7},{5,4},{6,5},{7,6},{8,11},{9,8},{10,9... | collective-permute-start | bytes 786440 | tf_op jit(solution)/shard_map/ppermute | solution.py:28
  15.7 5.2 %copy-start.3 = (bf16[8192,64]{0,1:T(8,128)(2,1)}, bf16[8192,64]{0,1:T(8,128)(2,1)S(1)}, u32[]{:S(2)}) copy-start(bf16[8192,64]{0,1:T(8,128)(2,1)S(1)} %constant_dynamic-update-slice_fusion.3) | copy-start | bytes 3145732
  21.8 11.4 %copy-start.6 = (s32[8192]{0:T(1024)S(1)}, s32[8192]{0:T(1024)}, u32[]{:S(2)}) copy-start(s32[8192]{0:T(1024)} %param.13) | copy-start | bytes 98308
  27.6 6.9 %collective-permute-start.2 = (bf16[64,128,16]{1,2,0:T(8,128)(2,1)S(1)}, bf16[64,128,16]{1,2,0:T(8,128)(2,1)S(1)}, u32[]{:S(2)}, u32[]{:S(2)}) collective-permute-start(bf16[64,128,16]{1,2,0:T(8,128)(2,1)S(1)} %copy_bitcast_fusion.1), channel_id=1, source_target_pairs={{0,4},{4,8},{8,12},{12,16},{16,20},{20,24},{24,28},{28,32},{32,36}... | collective-permute-start | bytes 786440 | tf_op jit(solution)/shard_map/ppermute | solution.py:43
  31.8 5.2 %collective-permute-start.3 = (bf16[64,128,16]{1,2,0:T(8,128)(2,1)S(1)}, bf16[64,128,16]{1,2,0:T(8,128)(2,1)S(1)}, u32[]{:S(2)}, u32[]{:S(2)}) collective-permute-start(bf16[64,128,16]{1,2,0:T(8,128)(2,1)S(1)} %copy_bitcast_fusion.1), channel_id=1, source_target_pairs={{4,0},{8,4},{12,8},{16,12},{20,16},{24,20},{28,24},{32,28},{36,32}... | collective-permute-start | bytes 786440 | tf_op jit(solution)/shard_map/ppermute | solution.py:44
  33.2 204.1 %collective-permute-start.16 = (bf16[8192,16]{0,1:T(8,128)(2,1)}, bf16[8192,16]{0,1:T(8,128)(2,1)}, u32[]{:S(2)}, u32[]{:S(2)}) collective-permute-start(bf16[8192,16]{0,1:T(8,128)(2,1)} %collective-permute-done.14), channel_id=1, source_target_pairs={{0,1},{1,2},{2,3},{3,0},{4,5},{5,6},{6,7},{7,4},{8,9},{9,10},{10,1... | collective-permute-start | bytes 786440 | tf_op jit(solution)/shard_map/ppermute | solution.py:23
  43.6 47.3 %copy-start.1 = (bf16[8,3,128,128]{3,2,1,0:T(8,128)(2,1)S(1)}, bf16[8,3,128,128]{3,2,1,0:T(8,128)(2,1)}, u32[]{:S(2)}) copy-start(bf16[8,3,128,128]{3,2,1,0:T(8,128)(2,1)} %param.12) | copy-start | bytes 2359300
  91.2 8.6 %collective-permute-start.5 = (bf16[1,128,16]{1,2,0:T(8,128)(2,1)S(1)}, bf16[1,128,16]{1,2,0:T(8,128)(2,1)S(1)}, u32[]{:S(2)}, u32[]{:S(2)}) collective-permute-start(bf16[1,128,16]{1,2,0:T(8,128)(2,1)S(1)} %get-tuple-element.19), channel_id=1, source_target_pairs={{4,0},{8,4},{12,8},{16,12},{20,16},{24,20},{28,24},{32,28},{36,32}... | collective-permute-start | bytes 12296 | tf_op jit(solution)/shard_map/ppermute | solution.py:44
  92.5 8.1 %collective-permute-start.4 = (bf16[1,128,16]{1,2,0:T(8,128)(2,1)S(1)}, bf16[1,128,16]{1,2,0:T(8,128)(2,1)S(1)}, u32[]{:S(2)}, u32[]{:S(2)}) collective-permute-start(bf16[1,128,16]{1,2,0:T(8,128)(2,1)S(1)} %get-tuple-element.18), channel_id=1, source_target_pairs={{0,4},{4,8},{8,12},{12,16},{16,20},{20,24},{24,28},{28,32},{32,36}... | collective-permute-start | bytes 12296 | tf_op jit(solution)/shard_map/ppermute | solution.py:43
  101.2 5.7 %collective-permute-start.7 = (bf16[1,128,16]{1,2,0:T(8,128)(2,1)S(1)}, bf16[1,128,16]{1,2,0:T(8,128)(2,1)S(1)}, u32[]{:S(2)}, u32[]{:S(2)}) collective-permute-start(bf16[1,128,16]{1,2,0:T(8,128)(2,1)S(1)} %get-tuple-element.17), channel_id=1, source_target_pairs={{4,0},{8,4},{12,8},{16,12},{20,16},{24,20},{28,24},{32,28},{36,32}... | collective-permute-start | bytes 12296 | tf_op jit(solution)/shard_map/ppermute | solution.py:44
  102.5 5.0 %collective-permute-start.6 = (bf16[1,128,16]{1,2,0:T(8,128)(2,1)S(1)}, bf16[1,128,16]{1,2,0:T(8,128)(2,1)S(1)}, u32[]{:S(2)}, u32[]{:S(2)}) collective-permute-start(bf16[1,128,16]{1,2,0:T(8,128)(2,1)S(1)} %get-tuple-element.16), channel_id=1, source_target_pairs={{0,4},{4,8},{8,12},{12,16},{16,20},{20,24},{24,28},{28,32},{32,36}... | collective-permute-start | bytes 12296 | tf_op jit(solution)/shard_map/ppermute | solution.py:43
  115.3 69.1 %copy-start.2 = (f32[128,8192]{1,0:T(8,128)S(1)}, f32[128,8192]{1,0:T(8,128)}, u32[]{:S(2)}) copy-start(f32[128,8192]{1,0:T(8,128)} %param.15) | copy-start | bytes 12582916
  115.3 4.0 %collective-permute-start.8 = (f32[128,16]{1,0:T(8,128)S(1)}, f32[128,16]{1,0:T(8,128)S(1)}, u32[]{:S(2)}, u32[]{:S(2)}) collective-permute-start(f32[128,16]{1,0:T(8,128)S(1)} %slice_select_fusion), channel_id=1, source_target_pairs={{0,4},{4,0},{8,12},{12,8},{16,20},{20,16},{24,28},{28,24},{32,36},... | collective-permute-start | bytes 24584 | tf_op jit(solution)/shard_map/ppermute | solution.py:52
  191.0 2.1 collective-permute-start.9
  196.4 4.6 %collective-permute-start.11 = (bf16[1,128,16]{1,2,0:T(8,128)(2,1)S(1)}, bf16[1,128,16]{1,2,0:T(8,128)(2,1)S(1)}, u32[]{:S(2)}, u32[]{:S(2)}) collective-permute-start(bf16[1,128,16]{1,2,0:T(8,128)(2,1)S(1)} %get-tuple-element.15), channel_id=1, source_target_pairs={{4,0},{8,4},{12,8},{16,12},{20,16},{24,20},{28,24},{32,28},{36,32}... | collective-permute-start | bytes 12296 | tf_op jit(solution)/shard_map/ppermute | solution.py:44
  197.7 3.8 %collective-permute-start.10 = (bf16[1,128,16]{1,2,0:T(8,128)(2,1)S(1)}, bf16[1,128,16]{1,2,0:T(8,128)(2,1)S(1)}, u32[]{:S(2)}, u32[]{:S(2)}) collective-permute-start(bf16[1,128,16]{1,2,0:T(8,128)(2,1)S(1)} %get-tuple-element.14), channel_id=1, source_target_pairs={{0,4},{4,8},{8,12},{12,16},{16,20},{20,24},{24,28},{28,32},{32,36}... | collective-permute-start | bytes 12296 | tf_op jit(solution)/shard_map/ppermute | solution.py:43
  232.8 6.3 %collective-permute-start.12 = (bf16[64,128,16]{1,2,0:T(8,128)(2,1)S(1)}, bf16[64,128,16]{1,2,0:T(8,128)(2,1)S(1)}, u32[]{:S(2)}, u32[]{:S(2)}) collective-permute-start(bf16[64,128,16]{1,2,0:T(8,128)(2,1)S(1)} %copy_bitcast_fusion), channel_id=1, source_target_pairs={{0,4},{4,8},{8,12},{12,16},{16,20},{20,24},{24,28},{28,32},{32,36}... | collective-permute-start | bytes 786440 | tf_op jit(solution)/shard_map/ppermute | solution.py:43
  236.1 5.2 %collective-permute-start.13 = (bf16[64,128,16]{1,2,0:T(8,128)(2,1)S(1)}, bf16[64,128,16]{1,2,0:T(8,128)(2,1)S(1)}, u32[]{:S(2)}, u32[]{:S(2)}) collective-permute-start(bf16[64,128,16]{1,2,0:T(8,128)(2,1)S(1)} %copy_bitcast_fusion), channel_id=1, source_target_pairs={{4,0},{8,4},{12,8},{16,12},{20,16},{24,20},{28,24},{32,28},{36,32}... | collective-permute-start | bytes 786440 | tf_op jit(solution)/shard_map/ppermute | solution.py:44
  242.2 6.0 %copy-start.4 = (bf16[8192,64]{0,1:T(8,128)(2,1)S(1)}, bf16[8192,64]{0,1:T(8,128)(2,1)}, u32[]{:S(2)}) copy-start(bf16[8192,64]{0,1:T(8,128)(2,1)} %constant_dynamic-update-slice_fusion) | copy-start | bytes 3145732
  248.2 131.8 %copy-start.5 = (f32[8192,16]{0,1:T(8,128)}, f32[8192,16]{0,1:T(8,128)S(1)}, u32[]{:S(2)}) copy-start(f32[8192,16]{0,1:T(8,128)S(1)} %fusion.7) | copy-start | bytes 1572868
